TPU v7x, 32 devices: a whole 2x2x4 slice. The times are simulated.
32 devices in a mesh: seq: 2 (over y), fsdp: 16 (over z, x, core).
Axes of the slice: x: 2, y: 2, z: 4, core: 2. Of those that a mesh axis runs over, the one named last changes fastest.
Arguments:
- tokens: bfloat16 [16, 1024, 1024], P('fsdp', 'seq'), may hold values from -6 to 6
- blocks: int32 [16, 1024], P('fsdp'), may hold values from 0 to 7, never falling along the last dimension, each value on 1 to 256 neighbouring positions
- first_gain: bfloat16 [1024], P('fsdp'), may hold values from 0.5 to 1.5
- first_shift: bfloat16 [1024], P('fsdp'), may hold values from -1.5 to 1.5
- joint_weight: bfloat16 [1024, 3072], P('fsdp'), may hold values from -0.1875 to 0.1875
- joint_bias: bfloat16 [2, 1024], P(None, 'fsdp'), may hold values from -1.5 to 1.5
- output_weight: bfloat16 [1024, 1024], P('fsdp'), may hold values from -0.75 to 0.75
- output_bias: bfloat16 [1024], P('fsdp'), may hold values from -1.5 to 1.5
- second_gain: bfloat16 [1024], P('fsdp'), may hold values from 0.5 to 1.5
- second_shift: bfloat16 [1024], P('fsdp'), may hold values from -1.5 to 1.5
- upward_weight: bfloat16 [1024, 4096], P('fsdp'), may hold values from -0.1875 to 0.1875
- upward_bias: bfloat16 [4096], P('fsdp'), may hold values from -1.5 to 1.5
- downward_weight: bfloat16 [4096, 1024], P('fsdp'), may hold values from -0.125 to 0.125
- downward_bias: bfloat16 [1024], P('fsdp'), may hold values from -1.5 to 1.5
- cotangent: bfloat16 [16, 1024, 1024], P('fsdp', 'seq'), may hold values from -6 to 6
Outputs:
- result: bfloat16 [16, 1024, 1024], P('fsdp', 'seq')
- grad_tokens: float32 [16, 1024, 1024], P('fsdp', 'seq')
- grad_first_gain: float32 [1024], P('fsdp')
- grad_first_shift: float32 [1024], P('fsdp')
- grad_joint_weight: float32 [1024, 3072], P('fsdp')
- grad_joint_bias: float32 [2, 1024], P(None, 'fsdp')
- grad_output_weight: float32 [1024, 1024], P('fsdp')
- grad_output_bias: float32 [1024], P('fsdp')
- grad_second_gain: float32 [1024], P('fsdp')
- grad_second_shift: float32 [1024], P('fsdp')
- grad_upward_weight: float32 [1024, 4096], P('fsdp')
- grad_upward_bias: float32 [4096], P('fsdp')
- grad_downward_weight: float32 [4096, 1024], P('fsdp')
- grad_downward_bias: float32 [1024], P('fsdp')
Inputs may be any that keep to these rules, and one draw needn't show every extreme that they name: `blocks`: along each sequence the block number never falls; every block has 1 to 256 tokens, and one has exactly 256.
All inputs are finite; a program needn't handle non-finite values.
Results may differ from a plain program's by a relative error of at most 0.014.
Values may be sent and summed in bfloat16 or wider, within the bound.
No kernel may reach another device: no remote copies, remote signals or barrier semaphores. Data moves between devices by JAX's collectives and lax.ppermute only.
A program may use at most 192 MiB of HBM per device.

v0:
```python
import jax
import jax.numpy as jnp
from jax import lax
from jax.sharding import PartitionSpec as P

HEADS = 16
HEAD_DIM = 64
EPSILON = 1e-05


def scaled_norm(values, gain):
    center = values - jnp.mean(values, axis=-1, keepdims=True)
    spread = jnp.mean(center * center, axis=-1, keepdims=True)
    return center * lax.rsqrt(spread + EPSILON) * gain


def gelu_tanh(values):
    return jax.nn.gelu(values, approximate=True)


def matmul(left, right):
    return jnp.dot(left, right, preferred_element_type=jnp.float32)


def left_contract(left, right):
    return lax.dot_general(
        left, right, (((0,), (0,)), ((), ())), preferred_element_type=jnp.float32
    )


def right_contract(left, right):
    return lax.dot_general(
        left, right, (((1,), (1,)), ((), ())), preferred_element_type=jnp.float32
    )


def masked_scores(queries, keys_in, slope, distance, allowed):
    scores = right_contract(queries, keys_in) * HEAD_DIM ** (-0.5) - slope * distance
    return jnp.where(allowed, scores, -1e30)


def attend_heads(heads, slopes, distance, allowed):

    def one_head(packed):
        queries, keys_in, values_in, slope = packed
        scores = masked_scores(queries, keys_in, slope, distance, allowed)
        top_score = jnp.max(scores, axis=1, keepdims=True)
        totals = jnp.sum(jnp.exp(scores - top_score), axis=1, keepdims=True)
        log_total = top_score + jnp.log(totals)
        probs = jnp.exp(scores - log_total).astype(jnp.bfloat16)
        return (matmul(probs, values_in).astype(jnp.bfloat16), log_total[:, 0])

    return lax.map(one_head, (heads[0], heads[1], heads[2], slopes))


def attend_back(heads, log_totals, grad_heads, slopes, distance, allowed):

    def one_head(packed):
        queries, keys_in, values_in, log_total, grad_head, slope = packed
        scores = masked_scores(queries, keys_in, slope, distance, allowed)
        probs = jnp.exp(scores - log_total[:, None])
        grad_probs = right_contract(grad_head, values_in)
        inner = jnp.sum(probs * grad_probs, axis=1, keepdims=True)
        grad_scores = (probs * (grad_probs - inner)).astype(jnp.bfloat16)
        factor = HEAD_DIM ** (-0.5)
        grad_queries = matmul(grad_scores, keys_in) * factor
        grad_keys = left_contract(grad_scores, queries) * factor
        grad_values = left_contract(probs.astype(jnp.bfloat16), grad_head)
        return jnp.stack([grad_queries, grad_keys, grad_values]).astype(jnp.bfloat16)

    return lax.map(one_head, (heads[0], heads[1], heads[2], log_totals, grad_heads, slopes))


def per_device(
    tokens,
    blocks,
    first_gain,
    first_shift,
    joint_weight,
    joint_bias,
    output_weight,
    output_bias,
    second_gain,
    second_shift,
    upward_weight,
    upward_bias,
    downward_weight,
    downward_bias,
    cotangent,
):
    groups = lax.axis_size("seq")
    token_count = tokens.shape[1]
    model_width = tokens.shape[2]
    seq_length = token_count * groups
    local_heads = HEADS // groups
    group_width = model_width // groups
    inputs = tokens[0].astype(jnp.float32)
    attn_set = (
        lax.all_gather(first_gain, "fsdp", axis=0, tiled=True),
        lax.all_gather(first_shift, "fsdp", axis=0, tiled=True),
        lax.all_gather(joint_weight, "fsdp", axis=0, tiled=True),
        lax.all_gather(joint_bias, "fsdp", axis=1, tiled=True),
        lax.all_gather(output_weight, "fsdp", axis=0, tiled=True),
        lax.all_gather(output_bias, "fsdp", axis=0, tiled=True),
    )
    normed_one = (
        scaled_norm(inputs, attn_set[0].astype(jnp.float32)) + attn_set[1].astype(jnp.float32)
    ).astype(jnp.bfloat16)
    bias_full = jnp.concatenate(
        [attn_set[3][0], jnp.zeros((model_width,), jnp.bfloat16), attn_set[3][1]]
    ).astype(jnp.float32)
    joint = (matmul(normed_one, attn_set[2]) + bias_full).astype(jnp.bfloat16)
    joint = joint.reshape(token_count, 3, groups, group_width)
    heads = lax.all_to_all(joint, "seq", split_axis=2, concat_axis=0, tiled=True)
    heads = heads.reshape(seq_length, 3, local_heads, HEAD_DIM).transpose(1, 2, 0, 3)
    positions = jnp.arange(seq_length)
    distance = jnp.abs(positions[:, None] - positions[None, :]).astype(jnp.float32)
    block_row = blocks[0]
    allowed = block_row[None, :] <= block_row[:, None]
    head_index = lax.axis_index("seq") * local_heads + jnp.arange(local_heads)
    slopes = jnp.exp2(-8.0 * (head_index.astype(jnp.float32) + 1.0) / HEADS)
    attended, log_totals = attend_heads(heads, slopes, distance, allowed)
    flat_heads = attended.transpose(1, 0, 2).reshape(seq_length, 1, group_width)
    mixed = lax.all_to_all(flat_heads, "seq", split_axis=0, concat_axis=1, tiled=True).reshape(
        token_count, model_width
    )
    hidden = inputs + matmul(mixed, attn_set[4]) + attn_set[5].astype(jnp.float32)
    mlp_set = (
        lax.all_gather(second_gain, "fsdp", axis=0, tiled=True),
        lax.all_gather(second_shift, "fsdp", axis=0, tiled=True),
        lax.all_gather(upward_weight, "fsdp", axis=0, tiled=True),
        lax.all_gather(upward_bias, "fsdp", axis=0, tiled=True),
        lax.all_gather(downward_weight, "fsdp", axis=0, tiled=True),
        lax.all_gather(downward_bias, "fsdp", axis=0, tiled=True),
    )
    normed_two = (
        scaled_norm(hidden, mlp_set[0].astype(jnp.float32)) + mlp_set[1].astype(jnp.float32)
    ).astype(jnp.bfloat16)
    upward = matmul(normed_two, mlp_set[2]) + mlp_set[3].astype(jnp.float32)
    activated = gelu_tanh(upward).astype(jnp.bfloat16)
    output = hidden + matmul(activated, mlp_set[4]) + mlp_set[5].astype(jnp.float32)
    back_gain_two, back_upward, back_downward = (
        lax.all_gather(second_gain, "fsdp", axis=0, tiled=True),
        lax.all_gather(upward_weight, "fsdp", axis=0, tiled=True),
        lax.all_gather(downward_weight, "fsdp", axis=0, tiled=True),
    )
    grad_output = cotangent[0].astype(jnp.float32)
    grad_low = grad_output.astype(jnp.bfloat16)
    grad_down_bias = jnp.sum(grad_low.astype(jnp.float32), axis=0)
    grad_down_weight = left_contract(activated, grad_low)
    grad_act = right_contract(grad_low, back_downward)
    gelu_back = jax.vjp(gelu_tanh, upward)[1]
    grad_up = gelu_back(grad_act)[0].astype(jnp.bfloat16)
    grad_up_bias = jnp.sum(grad_up.astype(jnp.float32), axis=0)
    grad_up_weight = left_contract(normed_two, grad_up)
    grad_normed_two = right_contract(grad_up, back_upward)
    norm_two_back = jax.vjp(scaled_norm, hidden, back_gain_two.astype(jnp.float32))[1]
    grad_hidden_norm, grad_gain_two = norm_two_back(grad_normed_two)
    grad_shift_two = jnp.sum(grad_normed_two, axis=0)
    grad_hidden = grad_output + grad_hidden_norm
    back_gain_one, back_joint, back_output = (
        lax.all_gather(first_gain, "fsdp", axis=0, tiled=True),
        lax.all_gather(joint_weight, "fsdp", axis=0, tiled=True),
        lax.all_gather(output_weight, "fsdp", axis=0, tiled=True),
    )
    hidden_low = grad_hidden.astype(jnp.bfloat16)
    grad_out_bias = jnp.sum(hidden_low.astype(jnp.float32), axis=0)
    grad_out_weight = left_contract(mixed, hidden_low)
    grad_mixed = right_contract(hidden_low, back_output).astype(jnp.bfloat16)
    grad_mixed = grad_mixed.reshape(token_count, groups, group_width)
    grad_heads = lax.all_to_all(grad_mixed, "seq", split_axis=1, concat_axis=0, tiled=True)
    grad_heads = grad_heads.reshape(seq_length, local_heads, HEAD_DIM).transpose(1, 0, 2)
    grad_stack = attend_back(heads, log_totals, grad_heads, slopes, distance, allowed)
    grad_stack = grad_stack.transpose(2, 1, 0, 3).reshape(seq_length, 3, 1, group_width)
    grad_joint = lax.all_to_all(grad_stack, "seq", split_axis=0, concat_axis=2, tiled=True)
    grad_joint = grad_joint.reshape(token_count, 3 * model_width)
    joint_sums = jnp.sum(grad_joint.astype(jnp.float32), axis=0)
    grad_joint_bias = jnp.stack([joint_sums[:model_width], joint_sums[2 * model_width :]])
    grad_joint_weight = left_contract(normed_one, grad_joint)
    grad_normed_one = right_contract(grad_joint, back_joint)
    norm_one_back = jax.vjp(scaled_norm, inputs, back_gain_one.astype(jnp.float32))[1]
    grad_input_norm, grad_gain_one = norm_one_back(grad_normed_one)
    grad_shift_one = jnp.sum(grad_normed_one, axis=0)
    grad_inputs = grad_hidden + grad_input_norm
    every_sum = (
        lax.psum_scatter(grad_gain_one, "fsdp", scatter_dimension=0, tiled=True),
        lax.psum_scatter(grad_shift_one, "fsdp", scatter_dimension=0, tiled=True),
        lax.psum_scatter(grad_joint_weight, "fsdp", scatter_dimension=0, tiled=True),
        lax.psum_scatter(grad_joint_bias, "fsdp", scatter_dimension=1, tiled=True),
        lax.psum_scatter(grad_out_weight, "fsdp", scatter_dimension=0, tiled=True),
        lax.psum_scatter(grad_out_bias, "fsdp", scatter_dimension=0, tiled=True),
        lax.psum_scatter(grad_gain_two, "fsdp", scatter_dimension=0, tiled=True),
        lax.psum_scatter(grad_shift_two, "fsdp", scatter_dimension=0, tiled=True),
        lax.psum_scatter(grad_up_weight, "fsdp", scatter_dimension=0, tiled=True),
        lax.psum_scatter(grad_up_bias, "fsdp", scatter_dimension=0, tiled=True),
        lax.psum_scatter(grad_down_weight, "fsdp", scatter_dimension=0, tiled=True),
        lax.psum_scatter(grad_down_bias, "fsdp", scatter_dimension=0, tiled=True),
    )
    attn_sums = every_sum[:6]
    mlp_sums = every_sum[6:]
    totals = (
        lax.psum(attn_sums[0].astype(jnp.bfloat16), "seq").astype(jnp.float32),
        lax.psum(attn_sums[1].astype(jnp.bfloat16), "seq").astype(jnp.float32),
        lax.psum(attn_sums[2].astype(jnp.bfloat16), "seq").astype(jnp.float32),
        lax.psum(attn_sums[3].astype(jnp.bfloat16), "seq").astype(jnp.float32),
        lax.psum(attn_sums[4].astype(jnp.bfloat16), "seq").astype(jnp.float32),
        lax.psum(attn_sums[5].astype(jnp.bfloat16), "seq").astype(jnp.float32),
        lax.psum(mlp_sums[0].astype(jnp.bfloat16), "seq").astype(jnp.float32),
        lax.psum(mlp_sums[1].astype(jnp.bfloat16), "seq").astype(jnp.float32),
        lax.psum(mlp_sums[2].astype(jnp.bfloat16), "seq").astype(jnp.float32),
        lax.psum(mlp_sums[3].astype(jnp.bfloat16), "seq").astype(jnp.float32),
        lax.psum(mlp_sums[4].astype(jnp.bfloat16), "seq").astype(jnp.float32),
        lax.psum(mlp_sums[5].astype(jnp.bfloat16), "seq").astype(jnp.float32),
    )
    return (
        output.astype(jnp.bfloat16)[None],
        grad_inputs[None],
        totals[0],
        totals[1],
        totals[2],
        totals[3],
        totals[4],
        totals[5],
        totals[6],
        totals[7],
        totals[8],
        totals[9],
        totals[10],
        totals[11],
    )


def solution(mesh):
    in_specs = (
        P("fsdp", "seq", None),
        P("fsdp", None),
        P("fsdp"),
        P("fsdp"),
        P("fsdp", None),
        P(None, "fsdp"),
        P("fsdp", None),
        P("fsdp"),
        P("fsdp"),
        P("fsdp"),
        P("fsdp", None),
        P("fsdp"),
        P("fsdp", None),
        P("fsdp"),
        P("fsdp", "seq", None),
    )
    out_specs = (
        P("fsdp", "seq", None),
        P("fsdp", "seq", None),
        P("fsdp"),
        P("fsdp"),
        P("fsdp", None),
        P(None, "fsdp"),
        P("fsdp", None),
        P("fsdp"),
        P("fsdp"),
        P("fsdp"),
        P("fsdp", None),
        P("fsdp"),
        P("fsdp", None),
        P("fsdp"),
    )
    return jax.shard_map(
        per_device, mesh=mesh, in_specs=in_specs, out_specs=out_specs, check_vma=False
    )
```

profile of v0, /device:TPU:0, one launch (start us, length us, event | category | flops | bytes accessed | tf_op | source)
XLA Modules:
  0.0 1121.6 jit_solution(8430259839319301549)
XLA Ops:
  10.1 23.6 %all-gather = bf16[16,64,2]{1,2,0:T(2,128)(2,1)S(1)} all-gather(bf16[1,64,2]{1,2,0:T(2,128)(2,1)} %bitcast.245), channel_id=1, replica_groups=mesh['seq'=2,'fsdp'=16] {'fsdp'}, dimensions={0}, use_global_device_ids=true | all-gather | bytes 4352 | tf_op jit(solution)/shard_map/all_gather | solution.py:102
  38.8 59.6 %all-reduce.14 = (bf16[1024]{0:T(1024)(128)(2,1)S(1)}, bf16[1024]{0:T(1024)(128)(2,1)S(1)}, bf16[1024]{0:T(1024)(128)(2,1)S(1)}, bf16[1024]{0:T(1024)(128)(2,1)}...) all-reduce(bf16[1024]{0:T(1024)(128)(2,1)S(1)} %dynamic-update-slic, ...), channel_id=1, replica_groups=mesh['seq'=2,'fsdp'=16] {'fsdp'}, use_global_device_ids=true, to_apply=%add.1 | all-reduce | flops 6144 | bytes 24576
  98.5 8.1 add_convert_fusion
  106.7 8.3 reshape.247
  115.0 8.6 copy.73
  123.6 5.5 all-to-all-start
  129.2 31.7 %all-to-all-done = bf16[512,3,2,512]{0,3,1,2:T(8,128)(2,1)} async-done(((bf16[512,3,2,512]{0,3,1,2:T(8,128)(2,1)}), bf16[512,3,2,512]{0,3,1,2:T(8,128)(2,1)}, u32[]{:S(2)}, u32[]{:S(2)}) %all-to-all-start) | async-done | bytes 3145760 | tf_op jit(solution)/shard_map/all_to_all | solution.py:114
  160.9 6.8 copy.74
  167.7 6.1 reshape.248
  173.8 3.3 slice_bitcast_fusion
  178.9 1.8 copy.76
  180.6 2.0 copy.77
  182.7 47.9 %while.24 = (s32[]{:T(128)}, bf16[8,1024,64]{1,2,0:T(8,128)(2,1)}, f32[8,1024]{1,0:T(8,128)S(1)}, bf16[8,1024,64]{2,1,0:T(8,128)(2,1)}, bf16[8,1024,64]{2,1,0:T(...) while((s32[]{:T(128)}, bf16[8,1024,64]{1,2,0:T(8,128)(2,1)}, ...), condition=%wide.region_5.6_spmd.clone, body=%wide.region_2.5_spmd.clone.sunk | while | flops 282131456 | bytes 13548157 | solution.py:53
  183.3 3.2 fusion.152
  189.3 3.2 fusion.152
  195.2 3.2 fusion.152
  201.2 3.3 fusion.152
  207.3 3.2 fusion.152
  213.3 3.2 fusion.152
  219.2 3.2 fusion.152
  225.2 3.2 fusion.152
  231.2 3.4 reduce.7
  234.6 2.3 copy.99
  236.9 2.6 reshape.301
  239.5 4.4 all-to-all-start.1
  244.0 19.0 %all-gather.1 = bf16[16,1,256]{2,1,0:T(2,128)(2,1)S(1)} all-gather(bf16[1,1,256]{2,1,0:T(2,128)(2,1)S(1)} %reshape.275), channel_id=1, replica_groups=mesh['seq'=2,'fsdp'=16] {'fsdp'}, dimensions={0}, use_global_device_ids=true | all-gather | bytes 8704 | tf_op jit(solution)/shard_map/all_gather | solution.py:132
  263.0 2.0 reshape.302
  266.2 2.4 copy.79
  268.6 3.3 fusion.115
  272.3 10.6 fusion.109
  282.9 14.3 %convert_reduce_fusion = (f32[4096]{0:T(1024)}, bf16[512,4096]{1,0:T(8,128)(2,1)S(1)}) fusion(f32[512,4096]{1,0:T(8,128)} %fusion.109, f32[4096]{0:T(1024)S(1)} %bitcast.240, bf16[4096,1024]{1,0:T(8,128)(2,1)} %all-gather.13.cloned.1.call-done, bf16[1,512,1024]{2,1,0:T(8,128)(2,1)S(1)} %copy-done.6), kind=kOutput, calls=%fused_computation.72 | convolution fusion | flops 4343197696 | bytes 22052864 | tf_op jit(solution)/shard_map/dot_general | solution.py:32
  297.2 5.0 multiply_reduce_fusion.1
  307.9 3.6 all-to-all-start.2
  311.6 3.3 fusion.116
  315.0 10.9 all-to-all-done.2
  327.9 99.5 %while.25 = (s32[]{:T(128)}, bf16[8,3,1024,64]{2,3,0,1:T(8,128)(2,1)}, bf16[8,1024,64]{2,1,0:T(8,128)(2,1)}, bf16[8,1024,64]{2,1,0:T(8,128)(2,1)}, f32[8]{0:T(12...) while((s32[]{:T(128)}, ...), condition=%wide.region_12.13_spmd.clone, body=%wide.region_10.12_spmd.clone.sunk | while | flops 688323584 | bytes 34241164 | solution.py:71
  330.1 4.3 multiply_reduce_fusion.5
  342.6 4.3 multiply_reduce_fusion.5
  355.0 4.3 multiply_reduce_fusion.5
  367.5 4.3 multiply_reduce_fusion.5
  379.9 4.3 multiply_reduce_fusion.5
  392.3 4.3 multiply_reduce_fusion.5
  404.7 4.3 multiply_reduce_fusion.5
  417.1 4.3 multiply_reduce_fusion.5
  427.3 7.6 copy.87
  434.9 51.4 %all_to_all.60 = bf16[1024,3,1,512]{3,1,2,0:T(4,128)(2,1)S(1)} all-to-all(bf16[1024,3,1,512]{3,1,2,0:T(4,128)(2,1)} %copy.87), channel_id=1, replica_groups=mesh['seq'=2,'fsdp'=16] {'seq'}, dimensions={0} | all-to-all | bytes 6291456 | tf_op jit(solution)/shard_map/all_to_all | solution.py:175
  487.1 2.8 copy.89
  490.0 10.5 fusion.88
  500.8 16.2 %fusion.108 = f32[1024,4096]{1,0:T(8,128)} fusion(bf16[512,4096]{1,0:T(8,128)(2,1)} %copy-done.33, f32[512,1024]{1,0:T(8,128)} %copy-done.4, f32[1024]{0:T(1024)S(1)} %convert_element_type.192, f32[1024]{0:T(1024)S(1)} %convert_element_type.191, f32[512]{0:T(512)S(1)} %fusion.106, f32[512]{0:T(512)S(1)} %broadcast_multiply_fusion), kind=kOutput, calls=%fused_computation.153 | convolution fusion | flops 4297588736 | bytes 23080960 | tf_op jit(solution)/shard_map/dot_general | solution.py:26
  517.1 17.9 %fusion.91 = f32[4096,1024]{1,0:T(8,128)} fusion(bf16[1,512,1024]{2,1,0:T(8,128)(2,1)} %param.33, f32[512,4096]{1,0:T(8,128)} %fusion.109, f32[4096]{0:T(1024)S(1)} %bitcast.241), kind=kOutput, calls=%fused_computation.116 | convolution fusion | flops 4315938816 | bytes 26230784 | tf_op jit(solution)/shard_map/dot_general | solution.py:26
  538.8 12.9 %fusion.85 = bf16[1,512,1024]{2,1,0:T(8,128)(2,1)} fusion(f32[512,1024]{1,0:T(8,128)} %copy-done.4, bf16[4096,1024]{1,0:T(8,128)(2,1)} %all-gather.13.cloned.1.call-done, f32[1024]{0:T(1024)S(1)} %convert_element_type.196, f32[512,4096]{1,0:T(8,128)} %fusion.109, f32[4096]{0:T(1024)S(1)} %bitcast.242), kind=kOutput, calls=%fused_computation.109 | convolution fusion | flops 4317511680 | bytes 19943424 | tf_op jit(solution)/shard_map/dot_general | solution.py:22
  553.4 79.2 %reduce-scatter.8.cloned.1.call-done = f32[64,3072]{1,0:T(8,128)} async-done(((f32[1024,3072]{1,0:T(8,128)}), f32[64,3072]{1,0:T(8,128)}) %reduce-scatter.8.cloned.1.call-update) | async-done | bytes 786448 | tf_op jit(solution)/shard_map/reduce_scatter | solution.py:188
  632.6 1.9 convert_element_type.208
  634.5 178.8 %reduce-scatter.12.cloned.1.call-done = f32[64,4096]{1,0:T(8,128)} async-done(((f32[1024,4096]{1,0:T(8,128)}), f32[64,4096]{1,0:T(8,128)}) %reduce-scatter.12.cloned.1.call-update) | async-done | bytes 1048592 | tf_op jit(solution)/shard_map/reduce_scatter | solution.py:194
  813.4 2.1 convert_element_type.222
  815.4 178.5 %reduce-scatter.14.cloned.1.call-done = f32[256,1024]{1,0:T(8,128)} async-done(((f32[4096,1024]{1,0:T(8,128)}), f32[256,1024]{1,0:T(8,128)}) %reduce-scatter.14.cloned.1.call-update) | async-done | bytes 1048592 | tf_op jit(solution)/shard_map/reduce_scatter | solution.py:196
  993.9 2.1 convert_element_type.227
  996.1 6.9 fusion.110
  1004.8 2.1 convert_reduce_fusion.3
  1007.0 59.6 %all-reduce.13 = (bf16[1024]{0:T(1024)(128)(2,1)S(1)}, bf16[1024]{0:T(1024)(128)(2,1)S(1)}, bf16[1024]{0:T(1024)(128)(2,1)S(1)}, bf16[1024]{0:T(1024)(128)(2,1)S...) all-reduce(f32[1024]{0:T(1024)S(1)} %get-tuple-element.229, ...), channel_id=2, replica_groups=mesh['seq'=2,'fsdp'=16] {'fsdp'}, use_global_device_ids=true, to_apply=%region_16.17.clone | all-reduce | flops 10240 | bytes 61440
  1068.0 5.1 all-reduce.15
  1077.3 30.3 %all-reduce.19.cloned.1.call-done = (bf16[64,3072]{1,0:T(8,128)(2,1)}, bf16[64,1024]{1,0:T(8,128)(2,1)}, bf16[64,4096]{1,0:T(8,128)(2,1)}, bf16[256,1024]{1,0:T(8,128)(2,1)}) async-done(((bf16[64,3072]{1,0:T(8,128)(2,1)}, bf16[64,1024]{1,0:T(8,128)(2,1)}, bf16[64,4096]{1,0:T(8,128)(2,1)}, bf16[256,1024]{1,0:T(8,128)(2,1)}), (bf16[64,3072]{1,0:T(8,128)(2,1)}, bf16[64,1024]{1,0:T(8,128)(2,1)}, ...) | async-done | bytes 1572880 | tf_op jit(solution)/shard_map/psum | solution.py:204
  1107.6 2.0 convert_element_type.209
  1111.2 2.1 convert_element_type.223
  (276 shorter events, 121.5 us)
Async XLA Ops:
  7.2 29.0 %copy-start.23 = (u32[32]{0:T(128)S(1)}, u32[32]{0:T(128)}, u32[]{:S(2)}) copy-start(u32[32]{0:T(128)} %constant.97) | copy-start | bytes 388
  7.2 28.0 %copy-start = (bf16[1,512,1024]{2,1,0:T(8,128)(2,1)S(1)}, bf16[1,512,1024]{2,1,0:T(8,128)(2,1)}, u32[]{:S(2)}) copy-start(bf16[1,512,1024]{2,1,0:T(8,128)(2,1)} %param.19) | copy-start | bytes 3145732
  7.2 30.2 %copy-start.26 = (bf16[64]{0:T(256)(128)(2,1)S(1)}, bf16[64]{0:T(256)(128)(2,1)}, u32[]{:S(2)}) copy-start(bf16[64]{0:T(256)(128)(2,1)} %param.22) | copy-start | bytes 388
  7.2 30.5 %copy-start.27 = (bf16[64]{0:T(256)(128)(2,1)S(1)}, bf16[64]{0:T(256)(128)(2,1)}, u32[]{:S(2)}) copy-start(bf16[64]{0:T(256)(128)(2,1)} %param.21) | copy-start | bytes 388
  7.2 30.7 %copy-start.28 = (bf16[64]{0:T(256)(128)(2,1)S(1)}, bf16[64]{0:T(256)(128)(2,1)}, u32[]{:S(2)}) copy-start(bf16[64]{0:T(256)(128)(2,1)} %param.26) | copy-start | bytes 388
  7.2 30.9 %copy-start.29 = (bf16[64]{0:T(256)(128)(2,1)S(1)}, bf16[64]{0:T(256)(128)(2,1)}, u32[]{:S(2)}) copy-start(bf16[64]{0:T(256)(128)(2,1)} %param.32) | copy-start | bytes 388
  7.2 31.1 %copy-start.30 = (bf16[64]{0:T(256)(128)(2,1)S(1)}, bf16[64]{0:T(256)(128)(2,1)}, u32[]{:S(2)}) copy-start(bf16[64]{0:T(256)(128)(2,1)} %param.28) | copy-start | bytes 388
  7.3 31.4 %copy-start.31 = (bf16[64]{0:T(256)(128)(2,1)S(1)}, bf16[64]{0:T(256)(128)(2,1)}, u32[]{:S(2)}) copy-start(bf16[64]{0:T(256)(128)(2,1)} %param.27) | copy-start | bytes 388
  7.3 91.3 %all-gather.7.cloned.1.call-start = ((), (), s32[]{:S(2)}) async-start(), calls=%async_computation.9 | async-start | bytes 6684672 | tf_op jit(solution)/shard_map/all_gather | solution.py:101
  8.0 260.6 %all-gather.9.cloned.1.call-start = ((), (), s32[]{:S(2)}) async-start(), calls=%async_computation.10 | async-start | bytes 2228224 | tf_op jit(solution)/shard_map/all_gather | solution.py:103
  8.7 263.5 %all-gather.11.cloned.1.call-start = ((), (), s32[]{:S(2)}) async-start(), calls=%async_computation.11 | async-start | bytes 8912896 | tf_op jit(solution)/shard_map/all_gather | solution.py:131
  9.5 273.4 %all-gather.13.cloned.1.call-start = ((), (), s32[]{:S(2)}) async-start(), calls=%async_computation.12 | async-start | bytes 8912896 | tf_op jit(solution)/shard_map/all_gather | solution.py:133
  35.2 71.5 %copy-start.13 = (f32[512]{0:T(512)}, f32[512]{0:T(512)S(1)}, u32[]{:S(2)}) copy-start(f32[512]{0:T(512)S(1)} %broadcast_multiply_fusion.1) | copy-start | bytes 6148
  35.6 0.6 copy-start.17
  35.6 71.1 %copy-start.15 = (f32[512]{0:T(512)}, f32[512]{0:T(512)S(1)}, u32[]{:S(2)}) copy-start(f32[512]{0:T(512)S(1)} %fusion.105) | copy-start | bytes 6148
  98.5 8.2 copy-start.20
  98.5 8.2 copy-start.11
  123.6 37.3 %all-to-all-start = ((bf16[512,3,2,512]{0,3,1,2:T(8,128)(2,1)}), bf16[512,3,2,512]{0,3,1,2:T(8,128)(2,1)}, u32[]{:S(2)}, u32[]{:S(2)}) async-start(bf16[512,3,2,512]{0,3,1,2:T(8,128)(2,1)} %copy.73), calls=%async_computation | async-start | bytes 6291456 | tf_op jit(solution)/shard_map/all_to_all | solution.py:114
  178.9 3.8 copy-start.25
  230.6 8.9 copy-start.5
  234.6 9.4 copy-start.32
  239.5 23.5 %all-to-all-start.1 = ((bf16[2,2,131072]{2,1,0:T(2,128)(2,1)}), bf16[2,2,131072]{2,1,0:T(2,128)(2,1)}, u32[]{:S(2)}, u32[]{:S(2)}) async-start(bf16[2,2,131072]{2,1,0:T(2,128)(2,1)} %reshape.301), calls=%async_computation.1 | async-start | bytes 2097152 | tf_op jit(solution)/shard_map/all_to_all | solution.py:124
  271.8 30.4 %copy-start.4 = (f32[512,1024]{1,0:T(8,128)}, f32[512,1024]{1,0:T(8,128)S(1)}, u32[]{:S(2)}) copy-start(f32[512,1024]{1,0:T(8,128)S(1)} %get-tuple-element.313) | copy-start | bytes 6291460
  272.2 10.7 copy-start.6
  282.9 14.3 %copy-start.24 = (bf16[1024,4096]{1,0:T(8,128)(2,1)S(1)}, bf16[1024,4096]{1,0:T(8,128)(2,1)}, u32[]{:S(2)}) copy-start(bf16[1024,4096]{1,0:T(8,128)(2,1)} %all-gather.11.cloned.1.call-done) | copy-start | bytes 25165828
  297.2 5.0 copy-start.33
  302.9 1.3 copy-start.2
  302.9 2.4 copy-start.9
  306.6 5.0 copy-start.8
  307.9 17.9 %all-to-all-start.2 = ((bf16[512,2,512]{0,2,1:T(8,128)(2,1)}), bf16[512,2,512]{0,2,1:T(8,128)(2,1)S(1)}, u32[]{:S(2)}, u32[]{:S(2)}) async-start(bf16[512,2,512]{0,2,1:T(8,128)(2,1)} %bitcast.19), calls=%async_computation.2 | async-start | bytes 2097152 | tf_op jit(solution)/shard_map/all_to_all | solution.py:171
  311.5 240.2 %reduce-scatter.10.cloned.1.call-start = ((), (), s32[]{:S(2)}) async-start(), calls=%async_computation.14 | async-start | bytes 4456448 | tf_op jit(solution)/shard_map/reduce_scatter | solution.py:190
  314.9 317.7 %reduce-scatter.8.cloned.1.call-start = ((), (), s32[]{:S(2)}) async-start(), calls=%async_computation.13 | async-start | bytes 13369344 | tf_op jit(solution)/shard_map/reduce_scatter | solution.py:188
  487.1 2.9 copy-start.12
  487.1 2.9 copy-start.14
  487.1 2.9 copy-start.16
  487.1 2.9 copy-start.21
  500.5 312.8 %reduce-scatter.12.cloned.1.call-start = ((), (), s32[]{:S(2)}) async-start(), calls=%async_computation.15 | async-start | bytes 17825792 | tf_op jit(solution)/shard_map/reduce_scatter | solution.py:194
  517.0 476.9 %reduce-scatter.14.cloned.1.call-start = ((), (), s32[]{:S(2)}) async-start(), calls=%async_computation.16 | async-start | bytes 17825792 | tf_op jit(solution)/shard_map/reduce_scatter | solution.py:196
  535.0 0.7 copy-start.22
  535.0 532.1 %reduce-scatter.16.cloned.1.call-start = ((), (), s32[]{:S(2)}) async-start(), calls=%async_computation.17 | async-start | bytes 557056
  538.5 569.1 %all-reduce.19.cloned.1.call-start = ((), (), s32[]{:S(2)}) async-start(), calls=%async_computation.18 | async-start | bytes 3145728 | tf_op jit(solution)/shard_map/psum | solution.py:204
  551.7 444.4 %copy-start.1 = (bf16[1,512,1024]{2,1,0:T(8,128)(2,1)S(1)}, bf16[1,512,1024]{2,1,0:T(8,128)(2,1)}, u32[]{:S(2)}) copy-start(bf16[1,512,1024]{2,1,0:T(8,128)(2,1)} %param.19) | copy-start | bytes 3145732
  996.1 6.9 copy-start.18
  1003.0 1.6 copy-start.3
  1003.0 1.9 copy-start.7
  1004.8 2.1 copy-start.19
  1107.6 5.7 copy-start.10
Sparse Core Ops, SparseCore 0:
  10.4 64.7 all-gather.6
  77.3 40.1 all-gather.8
  119.6 72.9 all-gather.10
  194.7 72.9 all-gather.12
  315.8 70.6 reduce-scatter.9
  500.7 131.9 reduce-scatter.7
  636.7 176.6 reduce-scatter.11
  817.5 176.4 reduce-scatter.13
  998.1 55.2 reduce-scatter.15
  1056.8 50.7 all-reduce.18
where the time goes:
time: 1130 us; the launch traced here: 1120 us
  waiting for transfers between devices  512 us (45%)
  matrix products  227 us (20%)
  blocking collectives  218 us (19%)
  local copies, waits for them, and re-layouts  82.9 us (7%)
  other arithmetic  49.6 us (4%)
  between operations  17.2 us (2%)
  starting transfers between devices  14.4 us (1%)
    reduce_scatter x1, waiting for transfers between devices, per_device(): lax.psum_scatter(grad_up_weight, 'fsdp', scatter_dimension=0, tiled=True)  179 us
    reduce_scatter x1, waiting for transfers between devices, per_device(): lax.psum_scatter(grad_down_weight, 'fsdp', scatter_dimension=0, tiled=True)  178 us
    unnamed x2, blocking collectives  119 us
    dot_general x28, matrix products, right_contract(): lax.dot_general(left, right, (((1,), (1,)), ((), ())), preferred_element_...  100 us
    reduce_scatter x1, waiting for transfers between devices, per_device(): lax.psum_scatter(grad_joint_weight, 'fsdp', scatter_dimension=0, tiled=True)  79.2 us
    dot_general x20, matrix products, left_contract(): lax.dot_general(left, right, (((0,), (0,)), ((), ())), preferred_element_...  67.8 us
    dot_general x20, matrix products, matmul(): return jnp.dot(left, right, preferred_element_type=jnp.float32)  58.5 us
    all_to_all x1, blocking collectives, per_device(): lax.all_to_all(grad_stack, 'seq', split_axis=0, concat_axis=2, tiled=True)  51.4 us
  transfers between devices with their start and end apart: 13, of which 6 were waited for; matrix products, arithmetic and copies ran while one was open for 29% of the time, Pallas kernels for 0%

commit v1 on v0

--- a/solution.py
+++ b/solution.py
@@ -1,3 +1,4 @@
+import functools
 import jax
 import jax.numpy as jnp
 from jax import lax
@@ -6,6 +7,26 @@
 HEADS = 16
 HEAD_DIM = 64
 EPSILON = 1e-05
+
+
+def racks_wait(field_in, bus_axis, along_dim):
+    count_all = lax.axis_size(bus_axis)
+    pile = tuple(((no, (no + 1) % count_all) for no in range(count_all)))
+    tray = tuple(((no, (no - 1) % count_all) for no in range(count_all)))
+    carry, state_now = ([field_in], [field_in])
+    for _ in range(count_all // 2):
+        item_now = lax.ppermute(carry[-1], bus_axis, pile)
+        carry.append(item_now)
+    i0 = 0
+    while i0 < (count_all - 1) // 2:
+        state_now.append(lax.ppermute(state_now[-1], bus_axis, tray))
+        i0 += 1
+    now = jnp.concatenate([*carry[::-1], *state_now[1:]], along_dim)
+    x_now = lax.axis_index(bus_axis)
+    return jnp.roll(now, (x_now - count_all // 2) * field_in.shape[along_dim], along_dim)
+
+
+step_on_tails_here = functools.partial(racks_wait, bus_axis="fsdp", along_dim=1)
 
 
 def scaled_norm(values, gain):
@@ -99,7 +120,7 @@
         lax.all_gather(first_gain, "fsdp", axis=0, tiled=True),
         lax.all_gather(first_shift, "fsdp", axis=0, tiled=True),
         lax.all_gather(joint_weight, "fsdp", axis=0, tiled=True),
-        lax.all_gather(joint_bias, "fsdp", axis=1, tiled=True),
+        step_on_tails_here(joint_bias),
         lax.all_gather(output_weight, "fsdp", axis=0, tiled=True),
         lax.all_gather(output_bias, "fsdp", axis=0, tiled=True),
     )

time: 1130 us -> 1150 us (1.018)
  starting transfers between devices: 14.4 us -> 46.6 us
  blocking collectives: 218 us -> 194 us
  waiting for transfers between devices: 512 us -> 527 us
    ppermute x0 -> x15, starting transfers between devices: none -> 32.2 us  [the longest x7 31.6 us: racks_wait(): state_now.append(lax.ppermute(state_now[-1], bus_axis, tray))]
    all_gather x1 -> x0, blocking collectives: 23.6 us -> none  [per_device(): lax.all_gather(joint_bias, 'fsdp', axis=1, tiled=True)]
    ppermute x0 -> x15, waiting for transfers between devices: none -> 13.3 us  [the longest x8 12.9 us: racks_wait(): item_now = lax.ppermute(carry[-1], bus_axis, pile)]
  transfers between devices with their start and end apart: 13 -> 28, of which waited for: 6 -> 17; matrix products, arithmetic and copies ran while one was open for 29% -> 28% of each run, Pallas kernels for 0% -> 0%
where the time goes in v1:
time: 1150 us; the launch traced here: 1140 us
  waiting for transfers between devices  527 us (46%)
  matrix products  226 us (20%)
  blocking collectives  194 us (17%)
  local copies, waits for them, and re-layouts  82.7 us (7%)
  other arithmetic  49.7 us (4%)
  starting transfers between devices  46.6 us (4%)
  between operations  17 us (1%)
    reduce_scatter x1, waiting for transfers between devices, per_device(): lax.psum_scatter(grad_up_weight, 'fsdp', scatter_dimension=0, tiled=True)  179 us
    reduce_scatter x1, waiting for transfers between devices, per_device(): lax.psum_scatter(grad_down_weight, 'fsdp', scatter_dimension=0, tiled=True)  179 us
    unnamed x2, blocking collectives  120 us
    dot_general x28, matrix products, right_contract(): lax.dot_general(left, right, (((1,), (1,)), ((), ())), preferred_element_...  100 us
    reduce_scatter x1, waiting for transfers between devices, per_device(): lax.psum_scatter(grad_joint_weight, 'fsdp', scatter_dimension=0, tiled=True)  80.7 us
    dot_general x20, matrix products, left_contract(): lax.dot_general(left, right, (((0,), (0,)), ((), ())), preferred_element_...  67.2 us
    dot_general x20, matrix products, matmul(): return jnp.dot(left, right, preferred_element_type=jnp.float32)  58.3 us
    all_to_all x1, blocking collectives, per_device(): lax.all_to_all(grad_stack, 'seq', split_axis=0, concat_axis=2, tiled=True)  51.4 us
  transfers between devices with their start and end apart: 28, of which 17 were waited for; matrix products, arithmetic and copies ran while one was open for 28% of the time, Pallas kernels for 0%

profile of v1, /device:TPU:0, one launch (start us, length us, event | category | flops | bytes accessed | tf_op | source)
XLA Modules:
  0.0 1143.6 jit_solution(2436061645783193778)
XLA Ops:
  10.1 5.0 collective-permute-start.8
  19.7 60.9 %all-reduce.14 = (bf16[1024]{0:T(1024)(128)(2,1)S(1)}, bf16[1024]{0:T(1024)(128)(2,1)S(1)}, bf16[1024]{0:T(1024)(128)(2,1)S(1)}, bf16[1024]{0:T(1024)(128)(2,1)}...) all-reduce(bf16[1024]{0:T(1024)(128)(2,1)S(1)} %dynamic-update-slic, ...), channel_id=1, replica_groups=mesh['seq'=2,'fsdp'=16] {'fsdp'}, use_global_device_ids=true, to_apply=%add.1 | all-reduce | flops 6144 | bytes 24576
  80.6 4.4 collective-permute-start.9
  86.4 4.4 collective-permute-start.10
  92.1 4.4 collective-permute-start.11
  97.8 4.4 collective-permute-start.12
  103.5 4.5 collective-permute-start.13
  109.3 4.4 collective-permute-start.14
  115.0 5.6 collective-permute-done.7
  120.8 7.9 add_convert_fusion
  128.8 8.3 reshape.247
  137.0 8.7 copy.69
  145.7 5.7 all-to-all-start
  151.4 32.0 %all-to-all-done = bf16[512,3,2,512]{0,3,1,2:T(8,128)(2,1)} async-done(((bf16[512,3,2,512]{0,3,1,2:T(8,128)(2,1)}), bf16[512,3,2,512]{0,3,1,2:T(8,128)(2,1)}, u32[]{:S(2)}, u32[]{:S(2)}) %all-to-all-start) | async-done | bytes 3145760 | tf_op jit(solution)/shard_map/all_to_all | solution.py:135
  183.4 6.8 copy.70
  190.2 6.2 reshape.248
  196.4 3.3 slice_bitcast_fusion
  205.3 47.9 %while.24 = (s32[]{:T(128)}, bf16[8,1024,64]{1,2,0:T(8,128)(2,1)}, f32[8,1024]{1,0:T(8,128)S(1)}, bf16[8,1024,64]{2,1,0:T(8,128)(2,1)}, bf16[8,1024,64]{2,1,0:T(...) while((s32[]{:T(128)}, bf16[8,1024,64]{1,2,0:T(8,128)(2,1)}, ...), condition=%wide.region_5.6_spmd.clone, body=%wide.region_2.5_spmd.clone.sunk | while | flops 282131456 | bytes 13548157 | solution.py:74
  205.9 3.2 fusion.152
  211.9 3.2 fusion.152
  217.9 3.2 fusion.152
  223.9 3.2 fusion.152
  229.8 3.2 fusion.152
  235.8 3.2 fusion.152
  241.8 3.2 fusion.152
  247.8 3.2 fusion.152
  253.7 3.3 reduce.7
  257.1 2.3 copy.95
  259.4 2.6 reshape.299
  262.0 4.4 all-to-all-start.1
  266.5 17.3 %all-gather = bf16[16,1,256]{2,1,0:T(2,128)(2,1)S(1)} all-gather(bf16[1,1,256]{2,1,0:T(2,128)(2,1)S(1)} %reshape.273), channel_id=1, replica_groups=mesh['seq'=2,'fsdp'=16] {'fsdp'}, dimensions={0}, use_global_device_ids=true | all-gather | bytes 8704 | tf_op jit(solution)/shard_map/all_gather | solution.py:153
  287.1 2.3 copy.75
  289.3 3.3 fusion.115
  293.0 10.7 fusion.109
  303.7 14.0 %convert_reduce_fusion = (f32[4096]{0:T(1024)}, bf16[512,4096]{1,0:T(8,128)(2,1)S(1)}) fusion(f32[512,4096]{1,0:T(8,128)} %fusion.109, f32[4096]{0:T(1024)S(1)} %bitcast.233, bf16[4096,1024]{1,0:T(8,128)(2,1)} %all-gather.12.cloned.1.call-done, bf16[1,512,1024]{2,1,0:T(8,128)(2,1)S(1)} %copy-done.6), kind=kOutput, calls=%fused_computation.72 | convolution fusion | flops 4343197696 | bytes 22052864 | tf_op jit(solution)/shard_map/dot_general | solution.py:53
  317.7 5.0 multiply_reduce_fusion.1
  328.4 3.6 all-to-all-start.2
  332.1 3.3 fusion.116
  335.5 11.1 all-to-all-done.2
  348.9 99.7 %while.25 = (s32[]{:T(128)}, bf16[8,3,1024,64]{2,3,0,1:T(8,128)(2,1)}, bf16[8,1024,64]{2,1,0:T(8,128)(2,1)}, bf16[8,1024,64]{2,1,0:T(8,128)(2,1)}, f32[8]{0:T(12...) while((s32[]{:T(128)}, ...), condition=%wide.region_12.13_spmd.clone, body=%wide.region_10.12_spmd.clone.sunk | while | flops 688323584 | bytes 34241164 | solution.py:92
  351.1 4.3 multiply_reduce_fusion.5
  363.6 4.4 multiply_reduce_fusion.5
  376.2 4.3 multiply_reduce_fusion.5
  388.6 4.3 multiply_reduce_fusion.5
  401.0 4.3 multiply_reduce_fusion.5
  413.5 4.3 multiply_reduce_fusion.5
  425.9 4.3 multiply_reduce_fusion.5
  438.4 4.3 multiply_reduce_fusion.5
  448.6 7.6 copy.83
  456.2 51.4 %all_to_all.60 = bf16[1024,3,1,512]{3,1,2,0:T(4,128)(2,1)S(1)} all-to-all(bf16[1024,3,1,512]{3,1,2,0:T(4,128)(2,1)} %copy.83), channel_id=1, replica_groups=mesh['seq'=2,'fsdp'=16] {'seq'}, dimensions={0} | all-to-all | bytes 6291456 | tf_op jit(solution)/shard_map/all_to_all | solution.py:196
  508.4 2.9 copy.85
  511.3 10.5 fusion.88
  522.0 15.7 %fusion.108 = f32[1024,4096]{1,0:T(8,128)} fusion(bf16[512,4096]{1,0:T(8,128)(2,1)} %copy-done.34, f32[512,1024]{1,0:T(8,128)} %copy-done.4, f32[1024]{0:T(1024)S(1)} %convert_element_type.192, f32[1024]{0:T(1024)S(1)} %convert_element_type.191, f32[512]{0:T(512)S(1)} %fusion.106, f32[512]{0:T(512)S(1)} %broadcast_multiply_fusion), kind=kOutput, calls=%fused_computation.153 | convolution fusion | flops 4297588736 | bytes 23080960 | tf_op jit(solution)/shard_map/dot_general | solution.py:47
  537.8 17.8 %fusion.91 = f32[4096,1024]{1,0:T(8,128)} fusion(bf16[1,512,1024]{2,1,0:T(8,128)(2,1)} %param.33, f32[512,4096]{1,0:T(8,128)} %fusion.109, f32[4096]{0:T(1024)S(1)} %bitcast.234), kind=kOutput, calls=%fused_computation.116 | convolution fusion | flops 4315938816 | bytes 26230784 | tf_op jit(solution)/shard_map/dot_general | solution.py:47
  559.4 12.9 %fusion.85 = bf16[1,512,1024]{2,1,0:T(8,128)(2,1)} fusion(f32[512,1024]{1,0:T(8,128)} %copy-done.4, bf16[4096,1024]{1,0:T(8,128)(2,1)} %all-gather.12.cloned.1.call-done, f32[1024]{0:T(1024)S(1)} %convert_element_type.196, f32[512,4096]{1,0:T(8,128)} %fusion.109, f32[4096]{0:T(1024)S(1)} %bitcast.235), kind=kOutput, calls=%fused_computation.109 | convolution fusion | flops 4317511680 | bytes 19943424 | tf_op jit(solution)/shard_map/dot_general | solution.py:43
  574.0 80.7 %reduce-scatter.8.cloned.1.call-done = f32[64,3072]{1,0:T(8,128)} async-done(((f32[1024,3072]{1,0:T(8,128)}), f32[64,3072]{1,0:T(8,128)}) %reduce-scatter.8.cloned.1.call-update) | async-done | bytes 786448 | tf_op jit(solution)/shard_map/reduce_scatter | solution.py:209
  656.7 178.8 %reduce-scatter.12.cloned.1.call-done = f32[64,4096]{1,0:T(8,128)} async-done(((f32[1024,4096]{1,0:T(8,128)}), f32[64,4096]{1,0:T(8,128)}) %reduce-scatter.12.cloned.1.call-update) | async-done | bytes 1048592 | tf_op jit(solution)/shard_map/reduce_scatter | solution.py:215
  837.5 178.5 %reduce-scatter.14.cloned.1.call-done = f32[256,1024]{1,0:T(8,128)} async-done(((f32[4096,1024]{1,0:T(8,128)}), f32[256,1024]{1,0:T(8,128)}) %reduce-scatter.14.cloned.1.call-update) | async-done | bytes 1048592 | tf_op jit(solution)/shard_map/reduce_scatter | solution.py:217
  1016.1 2.1 convert_element_type.227
  1018.2 6.9 fusion.110
  1027.0 2.1 convert_reduce_fusion.3
  1029.1 59.6 %all-reduce.13 = (bf16[1024]{0:T(1024)(128)(2,1)S(1)}, bf16[1024]{0:T(1024)(128)(2,1)S(1)}, bf16[1024]{0:T(1024)(128)(2,1)S(1)}, bf16[1024]{0:T(1024)(128)(2,1)S...) all-reduce(f32[1024]{0:T(1024)S(1)} %get-tuple-element.229, ...), channel_id=2, replica_groups=mesh['seq'=2,'fsdp'=16] {'fsdp'}, use_global_device_ids=true, to_apply=%region_16.17.clone | all-reduce | flops 10240 | bytes 61440
  1090.1 5.1 all-reduce.15
  1099.4 30.4 %all-reduce.19.cloned.1.call-done = (bf16[64,3072]{1,0:T(8,128)(2,1)}, bf16[64,1024]{1,0:T(8,128)(2,1)}, bf16[64,4096]{1,0:T(8,128)(2,1)}, bf16[256,1024]{1,0:T(8,128)(2,1)}) async-done(((bf16[64,3072]{1,0:T(8,128)(2,1)}, bf16[64,1024]{1,0:T(8,128)(2,1)}, bf16[64,4096]{1,0:T(8,128)(2,1)}, bf16[256,1024]{1,0:T(8,128)(2,1)}), (bf16[64,3072]{1,0:T(8,128)(2,1)}, bf16[64,1024]{1,0:T(8,128)(2,1)}, ...) | async-done | bytes 1572880 | tf_op jit(solution)/shard_map/psum | solution.py:225
  (306 shorter events, 143.0 us)
Async XLA Ops:
  7.2 9.9 copy-start.24
  7.2 113.4 %copy-start.23 = (bf16[2,64]{1,0:T(2,128)(2,1)S(1)}, bf16[2,64]{1,0:T(2,128)(2,1)}, u32[]{:S(2)}) copy-start(bf16[2,64]{1,0:T(2,128)(2,1)} %param.24) | copy-start | bytes 772
  7.2 9.4 copy-start
  7.2 11.1 copy-start.27
  7.2 11.3 copy-start.28
  7.2 11.6 %copy-start.29 = (bf16[64]{0:T(256)(128)(2,1)S(1)}, bf16[64]{0:T(256)(128)(2,1)}, u32[]{:S(2)}) copy-start(bf16[64]{0:T(256)(128)(2,1)} %param.26) | copy-start | bytes 388
  7.2 11.8 %copy-start.30 = (bf16[64]{0:T(256)(128)(2,1)S(1)}, bf16[64]{0:T(256)(128)(2,1)}, u32[]{:S(2)}) copy-start(bf16[64]{0:T(256)(128)(2,1)} %param.32) | copy-start | bytes 388
  7.3 12.0 %copy-start.31 = (bf16[64]{0:T(256)(128)(2,1)S(1)}, bf16[64]{0:T(256)(128)(2,1)}, u32[]{:S(2)}) copy-start(bf16[64]{0:T(256)(128)(2,1)} %param.28) | copy-start | bytes 388
  7.3 12.2 %copy-start.32 = (bf16[64]{0:T(256)(128)(2,1)S(1)}, bf16[64]{0:T(256)(128)(2,1)}, u32[]{:S(2)}) copy-start(bf16[64]{0:T(256)(128)(2,1)} %param.27) | copy-start | bytes 388
  7.3 113.6 %all-gather.6.cloned.1.call-start = ((), (), s32[]{:S(2)}) async-start(), calls=%async_computation.9 | async-start | bytes 6684672 | tf_op jit(solution)/shard_map/all_gather | solution.py:122
  8.0 281.3 %all-gather.8.cloned.1.call-start = ((), (), s32[]{:S(2)}) async-start(), calls=%async_computation.10 | async-start | bytes 2228224 | tf_op jit(solution)/shard_map/all_gather | solution.py:124
  8.8 284.3 %all-gather.10.cloned.1.call-start = ((), (), s32[]{:S(2)}) async-start(), calls=%async_computation.11 | async-start | bytes 8912896 | tf_op jit(solution)/shard_map/all_gather | solution.py:152
  9.5 294.2 %all-gather.12.cloned.1.call-start = ((), (), s32[]{:S(2)}) async-start(), calls=%async_computation.12 | async-start | bytes 8912896 | tf_op jit(solution)/shard_map/all_gather | solution.py:154
  9.5 71.1 %collective-permute-start = (bf16[2,64]{1,0:T(2,128)(2,1)}, bf16[2,64]{1,0:T(2,128)(2,1)S(1)}, u32[]{:S(2)}, u32[]{:S(2)}) collective-permute-start(bf16[2,64]{1,0:T(2,128)(2,1)} %param.24), channel_id=1, source_target_pairs={{0,1},{1,2},{2,3},{3,4},{4,5},{5,6},{6,7},{7,8},{8,9},{9,10},{10,1... | collective-permute-start | bytes 776 | tf_op jit(solution)/shard_map/ppermute | solution.py:18
  10.1 70.5 %collective-permute-start.8 = (bf16[2,64]{1,0:T(2,128)(2,1)}, bf16[2,64]{1,0:T(2,128)(2,1)S(1)}, u32[]{:S(2)}, u32[]{:S(2)}) collective-permute-start(bf16[2,64]{1,0:T(2,128)(2,1)} %param.24), channel_id=1, source_target_pairs={{0,15},{1,0},{2,1},{3,2},{4,3},{5,4},{6,5},{7,6},{8,7},{9,8},{10,9... | collective-permute-start | bytes 776 | tf_op jit(solution)/shard_map/ppermute | solution.py:22
  16.6 112.2 %copy-start.13 = (f32[512]{0:T(512)}, f32[512]{0:T(512)S(1)}, u32[]{:S(2)}) copy-start(f32[512]{0:T(512)S(1)} %broadcast_multiply_fusion.1) | copy-start | bytes 6148
  17.0 97.9 %copy-start.17 = (f32[512]{0:T(512)}, f32[512]{0:T(512)S(1)}, u32[]{:S(2)}) copy-start(f32[512]{0:T(512)S(1)} %fusion.78) | copy-start | bytes 6148
  17.0 111.7 %copy-start.15 = (f32[512]{0:T(512)}, f32[512]{0:T(512)S(1)}, u32[]{:S(2)}) copy-start(f32[512]{0:T(512)S(1)} %fusion.105) | copy-start | bytes 6148
  80.6 5.7 collective-permute-start.1
  80.6 5.7 collective-permute-start.9
  86.3 5.7 collective-permute-start.2
  86.4 5.7 collective-permute-start.10
  92.0 5.7 collective-permute-start.3
  92.1 5.7 collective-permute-start.11
  97.7 5.7 collective-permute-start.4
  97.8 5.7 collective-permute-start.12
  103.4 5.8 collective-permute-start.5
  103.5 5.8 collective-permute-start.13
  109.2 5.7 collective-permute-start.6
  109.3 5.7 collective-permute-start.14
  114.9 5.7 collective-permute-start.7
  114.9 13.9 %copy-start.20 = (f32[1024]{0:T(1024)}, f32[1024]{0:T(1024)S(1)}, u32[]{:S(2)}) copy-start(f32[1024]{0:T(1024)S(1)} %convert_element_type.184) | copy-start | bytes 12292
  114.9 13.9 %copy-start.11 = (f32[1024]{0:T(1024)}, f32[1024]{0:T(1024)S(1)}, u32[]{:S(2)}) copy-start(f32[1024]{0:T(1024)S(1)} %convert_element_type.183) | copy-start | bytes 12292
  145.7 37.7 %all-to-all-start = ((bf16[512,3,2,512]{0,3,1,2:T(8,128)(2,1)}), bf16[512,3,2,512]{0,3,1,2:T(8,128)(2,1)}, u32[]{:S(2)}, u32[]{:S(2)}) async-start(bf16[512,3,2,512]{0,3,1,2:T(8,128)(2,1)} %copy.69), calls=%async_computation | async-start | bytes 6291456 | tf_op jit(solution)/shard_map/all_to_all | solution.py:135
  201.5 3.9 copy-start.26
  253.2 8.8 copy-start.5
  257.1 9.4 copy-start.33
  262.0 21.8 %all-to-all-start.1 = ((bf16[2,2,131072]{2,1,0:T(2,128)(2,1)}), bf16[2,2,131072]{2,1,0:T(2,128)(2,1)}, u32[]{:S(2)}, u32[]{:S(2)}) async-start(bf16[2,2,131072]{2,1,0:T(2,128)(2,1)} %reshape.299), calls=%async_computation.1 | async-start | bytes 2097152 | tf_op jit(solution)/shard_map/all_to_all | solution.py:145
  292.6 30.1 %copy-start.4 = (f32[512,1024]{1,0:T(8,128)}, f32[512,1024]{1,0:T(8,128)S(1)}, u32[]{:S(2)}) copy-start(f32[512,1024]{1,0:T(8,128)S(1)} %get-tuple-element.313) | copy-start | bytes 6291460
  293.0 10.7 copy-start.6
  303.7 14.0 %copy-start.25 = (bf16[1024,4096]{1,0:T(8,128)(2,1)S(1)}, bf16[1024,4096]{1,0:T(8,128)(2,1)}, u32[]{:S(2)}) copy-start(bf16[1024,4096]{1,0:T(8,128)(2,1)} %all-gather.10.cloned.1.call-done) | copy-start | bytes 25165828
  317.7 5.0 copy-start.34
  323.4 1.3 copy-start.2
  323.5 2.4 copy-start.9
  327.1 5.0 copy-start.8
  328.4 18.2 %all-to-all-start.2 = ((bf16[512,2,512]{0,2,1:T(8,128)(2,1)}), bf16[512,2,512]{0,2,1:T(8,128)(2,1)S(1)}, u32[]{:S(2)}, u32[]{:S(2)}) async-start(bf16[512,2,512]{0,2,1:T(8,128)(2,1)} %bitcast.16), calls=%async_computation.2 | async-start | bytes 2097152 | tf_op jit(solution)/shard_map/all_to_all | solution.py:192
  332.0 240.3 %reduce-scatter.10.cloned.1.call-start = ((), (), s32[]{:S(2)}) async-start(), calls=%async_computation.14 | async-start | bytes 4456448 | tf_op jit(solution)/shard_map/reduce_scatter | solution.py:211
  335.4 319.3 %reduce-scatter.8.cloned.1.call-start = ((), (), s32[]{:S(2)}) async-start(), calls=%async_computation.13 | async-start | bytes 13369344 | tf_op jit(solution)/shard_map/reduce_scatter | solution.py:209
  508.4 2.9 copy-start.12
  508.4 2.9 copy-start.14
  508.4 2.9 copy-start.16
  508.4 2.9 copy-start.21
  521.8 313.7 %reduce-scatter.12.cloned.1.call-start = ((), (), s32[]{:S(2)}) async-start(), calls=%async_computation.15 | async-start | bytes 17825792 | tf_op jit(solution)/shard_map/reduce_scatter | solution.py:215
  537.8 478.3 %reduce-scatter.14.cloned.1.call-start = ((), (), s32[]{:S(2)}) async-start(), calls=%async_computation.16 | async-start | bytes 17825792 | tf_op jit(solution)/shard_map/reduce_scatter | solution.py:217
  555.6 0.7 copy-start.22
  555.7 533.6 %reduce-scatter.16.cloned.1.call-start = ((), (), s32[]{:S(2)}) async-start(), calls=%async_computation.17 | async-start | bytes 557056
  559.2 570.6 %all-reduce.19.cloned.1.call-start = ((), (), s32[]{:S(2)}) async-start(), calls=%async_computation.18 | async-start | bytes 3145728 | tf_op jit(solution)/shard_map/psum | solution.py:225
  572.3 445.9 %copy-start.1 = (bf16[1,512,1024]{2,1,0:T(8,128)(2,1)S(1)}, bf16[1,512,1024]{2,1,0:T(8,128)(2,1)}, u32[]{:S(2)}) copy-start(bf16[1,512,1024]{2,1,0:T(8,128)(2,1)} %param.19) | copy-start | bytes 3145732
  1018.2 6.9 copy-start.18
  1025.1 1.6 copy-start.3
  1025.1 1.9 copy-start.7
  1027.0 2.1 copy-start.19
  1129.8 5.7 copy-start.10
Sparse Core Ops, SparseCore 0:
  10.4 64.6 all-gather.5
  77.3 40.1 all-gather.7
  119.7 73.0 all-gather.9
  194.8 72.9 all-gather.11
  336.4 71.8 reduce-scatter.9
  521.9 132.7 reduce-scatter.7
  658.9 176.5 reduce-scatter.11
  839.6 176.4 reduce-scatter.13
  1020.2 55.3 reduce-scatter.15
  1079.0 50.6 all-reduce.18
